TPU v7x, 256 devices: a whole 4x4x8 slice. The times are simulated.
256 devices in a mesh: dp: 32 (over x, y, core), mp: 8 (over z).
Axes of the slice: x: 4, y: 4, z: 8, core: 2. Of those that a mesh axis runs over, the one named last changes fastest.
Arguments:
- queries: bfloat16 [4096, 64, 128], P('dp', 'mp'), may hold values from -6 to 6
- key_cache: bfloat16 [4096, 8, 128, 128], P('dp', 'mp'), may hold values from -6 to 6
- value_cache: bfloat16 [4096, 8, 128, 128], P('dp', 'mp'), may hold values from -6 to 6
- key_new: bfloat16 [4096, 8, 128], P('dp', 'mp'), may hold values from -6 to 6
- value_new: bfloat16 [4096, 8, 128], P('dp', 'mp'), may hold values from -6 to 6
- lengths: int32 [4096], P('dp'), may hold values from 1 to 128, as said below
- occupied: int32 [4096], P('dp'), may hold values 0 or 1
- slot_request: int32 [4096], P('dp'), may hold values from 0 to 4095, as said below
- request_adapter: int32 [4096], replicated, may hold values from 0 to 63, as said below
- out_weight: bfloat16 [8192, 4096], P('mp'), may hold values from -0.375 to 0.375
- shrink_weight: bfloat16 [64, 8192, 64], P('dp', 'mp'), may hold values from -0.375 to 0.375
- expand_weight: bfloat16 [64, 64, 4096], P('dp', None, 'mp'), may hold values from -0.75 to 0.75
Outputs:
- mixed: bfloat16 [4096, 4096], P('dp', 'mp')
Inputs may be any that keep to these rules, and one draw needn't show every extreme that they name: `slot_request`: A permutation: each request stands in exactly one slot. `request_adapter`: adapter n is owned by dp index n // 2. Among the slots of one dp index, at most 8 hold requests whose adapters one dp index owns; in every draw some dp index owns the adapters of exactly 8 slots of every dp index. `lengths`: each dp index has a slot of length 128.
All inputs are finite; a program needn't handle non-finite values. No bound on the sum of `occupied` on one device may be relied on, other than what follows from the above.
Results may differ from a plain program's by a relative error of at most 0.011.
Values may be sent and summed in bfloat16 or wider, within the bound.
A program may use at most 64 MiB of HBM per device.

v0:
```python
import math
import jax
import jax.numpy as jnp
from jax import lax
from jax.sharding import PartitionSpec as P


def attend(queries, key_cache, value_cache, key_new, value_new, lengths):
    rows, heads, width = queries.shape
    kv_local = key_cache.shape[1]
    group = heads // kv_local
    inverse = 1.0 / math.sqrt(width)
    grouped = queries.reshape(rows, kv_local, group, width)
    cached = (
        jnp.einsum("bgjd,bgtd->bgjt", grouped, key_cache, preferred_element_type=jnp.float32)
        * inverse
    )
    fresh = (
        jnp.einsum("bgjd,bgd->bgj", grouped, key_new, preferred_element_type=jnp.float32) * inverse
    )
    valid = jnp.arange(key_cache.shape[2])[None, :] < lengths[:, None]
    cached = jnp.where(valid[:, None, None, :], cached, -jnp.inf)
    top = jnp.maximum(jnp.max(cached, axis=-1), fresh)
    cached_exp = jnp.exp(cached - top[..., None])
    fresh_exp = jnp.exp(fresh - top)
    total = jnp.sum(cached_exp, axis=-1) + fresh_exp
    cached_w = (cached_exp / total[..., None]).astype(jnp.bfloat16)
    fresh_w = (fresh_exp / total).astype(jnp.bfloat16)
    summed = jnp.einsum(
        "bgjt,bgtd->bgjd", cached_w, value_cache, preferred_element_type=jnp.float32
    )
    summed = (
        summed
        + fresh_w.astype(jnp.float32)[..., None] * value_new.astype(jnp.float32)[:, :, None, :]
    )
    return summed.reshape(rows, heads * width).astype(jnp.bfloat16)


def body(
    queries,
    key_cache,
    value_cache,
    key_new,
    value_new,
    lengths,
    occupied,
    slot_request,
    request_adapter,
    out_weight,
    shrink_weight,
    expand_weight,
):
    rows = queries.shape[0]
    attended = attend(queries, key_cache, value_cache, key_new, value_new, lengths)
    owners_count = lax.axis_size("dp")
    adapters_here = shrink_weight.shape[0]
    rank_width = shrink_weight.shape[2]
    out_local = expand_weight.shape[2]
    capacity = 2 * rows // owners_count
    matches = (
        slot_request[:, None] == jnp.arange(request_adapter.shape[0], dtype=jnp.int32)[None, :]
    )
    slot_adapter = jnp.sum(jnp.where(matches, request_adapter[None, :], 0), axis=1)
    owner = slot_adapter // adapters_here
    local_ids = slot_adapter % adapters_here
    owner_onehot = (owner[:, None] == jnp.arange(owners_count, dtype=jnp.int32)[None, :]).astype(
        jnp.int32
    )
    earlier = jnp.cumsum(owner_onehot, axis=0) - owner_onehot
    position = jnp.sum(earlier * owner_onehot, axis=1)
    slot_code = owner * capacity + position
    dispatch = jnp.arange(owners_count * capacity, dtype=jnp.int32)[:, None] == slot_code[None, :]
    send_rows = jnp.dot(
        dispatch.astype(jnp.bfloat16), attended, preferred_element_type=jnp.float32
    ).astype(jnp.bfloat16)
    send_rows = send_rows.reshape(owners_count, capacity, attended.shape[1])
    send_ids = jnp.sum(jnp.where(dispatch, (local_ids + 1)[None, :], 0), axis=1).reshape(
        owners_count, capacity
    )
    combine = (
        slot_code[:, None] == jnp.arange(owners_count * capacity, dtype=jnp.int32)[None, :]
    ).astype(jnp.bfloat16)
    partial_value = jnp.dot(attended, out_weight, preferred_element_type=jnp.float32)
    full = lax.psum(partial_value, "mp")
    base = lax.dynamic_slice_in_dim(full, lax.axis_index("mp") * out_local, out_local, 1)
    got_rows = lax.all_to_all(send_rows, "dp", split_axis=0, concat_axis=0, tiled=True)
    got_ids = lax.all_to_all(send_ids, "dp", split_axis=0, concat_axis=0, tiled=True)
    flat = got_rows.reshape(owners_count * capacity, got_rows.shape[2])
    wanted = got_ids.reshape(owners_count * capacity) - 1
    partial_value = jnp.einsum(
        "md,adr->mar", flat, shrink_weight, preferred_element_type=jnp.float32
    )
    which = jnp.arange(adapters_here, dtype=jnp.int32)[None, :] == wanted[:, None]
    partial_value = jnp.where(which[:, :, None], partial_value, 0.0)
    summed = lax.psum(
        partial_value.reshape(owners_count * capacity, adapters_here * rank_width), "mp"
    )
    low = summed.astype(jnp.bfloat16).reshape(owners_count * capacity, adapters_here, rank_width)
    delta = 0.5 * jnp.einsum("mar,are->me", low, expand_weight, preferred_element_type=jnp.float32)
    delta = delta.astype(jnp.bfloat16).reshape(owners_count, capacity, out_local)
    back = lax.all_to_all(delta, "dp", split_axis=0, concat_axis=0, tiled=True)
    correction = jnp.dot(
        combine,
        back.reshape(owners_count * capacity, out_local),
        preferred_element_type=jnp.float32,
    )
    return (occupied.astype(jnp.float32)[:, None] * (base + correction)).astype(jnp.bfloat16)


def solution(mesh):
    placed = (
        P("dp", "mp", None),
        P("dp", "mp", None, None),
        P("dp", "mp", None, None),
        P("dp", "mp", None),
        P("dp", "mp", None),
        P("dp"),
        P("dp"),
        P("dp"),
        P(),
        P("mp", None),
        P("dp", "mp", None),
        P("dp", None, "mp"),
    )
    return jax.shard_map(body, mesh=mesh, in_specs=placed, out_specs=P("dp", "mp"), check_vma=False)
```

profile of v0, /device:TPU:22, one launch (start us, length us, event | category | flops | bytes accessed | tf_op | source)
XLA Modules:
  0.0 117.1 jit_solution(17132844115245272164)
XLA Ops:
  6.5 0.0 copy-start
  6.5 0.0 copy-start.1
  6.5 0.0 copy-start.6
  6.5 0.0 copy-start.3
  6.5 0.0 all-reduce.3.cloned.1.call-start
  6.6 0.8 iota_compare_fusion.6
  7.4 4.6 %fusion.42 = (f32[128,8]{1,0:T(8,128)S(1)}, f32[128,8,128]{2,1,0:T(8,128)S(1)}) fusion(bf16[128,8,128]{2,1,0:T(8,128)(2,1)} %param.12, bf16[128,1,128,128]{3,2,1,0:T(8,128)(2,1)} %param.13, pred[128,128]{1,0:T(8,128)(4,1)S(1)} %iota_compare_fusion.6), kind=kOutput, calls=%fused_computation.60 | convolution fusion | flops 33946624 | bytes 5001216 | tf_op jit(solution)/shard_map/bgjd,bgtd->bgjt/dot_general | solution.py:15
  12.0 0.1 copy.19
  12.1 0.0 copy-done.1
  12.1 0.0 copy-done.6
  12.1 0.3 fusion.36
  12.4 0.1 copy.20
  12.6 0.4 fusion.24
  13.0 0.1 copy.22
  13.1 0.1 copy.23
  13.2 0.0 copy-done.3
  13.3 3.5 %fusion.16 = bf16[128,8,128]{2,1,0:T(8,128)(2,1)S(1)} fusion(bf16[128,1,128,128]{3,2,1,0:T(8,128)(2,1)} %param.14, f32[128,8,128]{2,1,0:T(8,128)S(1)} %get-tuple-element.10, f32[128,128]{1,0:T(8,128)S(1)} %bitcast_convert_fusion, f32[128,8]{1,0:T(8,128)S(1)} %copy.23, f32[128,8]{1,0:T(8,128)S(1)} %copy.22, f32[128,8]{1,0:T(8,128)S(1)} %copy.20), kind=kOutput, calls=%fused_computation.14 | convolution fusion | flops 34340864 | bytes 5058560 | tf_op jit(solution)/shard_map/bgjt,bgtd->bgjd/dot_general | solution.py:29
  16.7 0.0 copy-start.4
  16.7 0.0 copy-start.5
  16.7 6.0 %fusion.26 = f32[128,4096]{1,0:T(8,128)} fusion(bf16[1024,4096]{1,0:T(8,128)(2,1)} %param.21, bf16[16,8,8,128]{3,2,1,0:T(8,128)(2,1)S(1)} %bitcast.75), kind=kOutput, calls=%fused_computation.25 | convolution fusion | flops 1073741824 | bytes 10747904 | tf_op jit(solution)/shard_map/dot_general | solution.py:83
  22.7 0.0 copy-start.2
  22.7 0.0 copy-start.7
  22.7 0.0 all-reduce.3.cloned.1.call-update
  22.7 0.0 copy-done.4
  22.8 0.0 copy-done.5
  22.8 0.4 select_reduce_fusion
  23.2 0.1 fusion.35
  23.3 0.2 reduce_window_sum.11
  23.5 0.2 select_reduce_fusion.2
  23.7 0.1 select_reduce_fusion.1
  23.8 0.7 all_to_all.12
  24.5 7.4 %all-to-all-start = ((s32[32,1,8]{2,1,0:T(1,128)}), s32[32,1,8]{2,1,0:T(1,128)S(1)}, u32[]{:S(2)}, u32[]{:S(2)}) async-start(s32[32,1,8]{2,1,0:T(1,128)} %bitcast.6), calls=%async_computation | async-start | bytes 32768 | tf_op jit(solution)/shard_map/all_to_all | solution.py:87
  31.9 1.1 fusion.4
  33.0 2.5 %all-to-all-done = s32[32,1,8]{2,1,0:T(1,128)S(1)} async-done(((s32[32,1,8]{2,1,0:T(1,128)}), s32[32,1,8]{2,1,0:T(1,128)S(1)}, u32[]{:S(2)}, u32[]{:S(2)}) %all-to-all-start) | async-done | bytes 1056 | tf_op jit(solution)/shard_map/all_to_all | solution.py:87
  35.4 7.6 %all-to-all-start.1 = ((bf16[32,8,1024]{2,1,0:T(8,128)(2,1)}), bf16[32,8,1024]{2,1,0:T(8,128)(2,1)S(1)}, u32[]{:S(2)}, u32[]{:S(2)}) async-start(bf16[32,8,1024]{2,1,0:T(8,128)(2,1)} %fusion.4), calls=%async_computation.1 | async-start | bytes 1048576 | tf_op jit(solution)/shard_map/all_to_all | solution.py:86
  43.1 0.1 sub.34
  43.2 7.9 %all-to-all-done.1 = bf16[32,8,1024]{2,1,0:T(8,128)(2,1)S(1)} async-done(((bf16[32,8,1024]{2,1,0:T(8,128)(2,1)}), bf16[32,8,1024]{2,1,0:T(8,128)(2,1)S(1)}, u32[]{:S(2)}, u32[]{:S(2)}) %all-to-all-start.1) | async-done | bytes 524320 | tf_op jit(solution)/shard_map/all_to_all | solution.py:86
  51.1 0.0 copy-done
  51.1 0.3 fusion.22
  51.5 34.2 %all-reduce.4 = bf16[256,128]{0,1:T(8,128)(2,1)S(1)} all-reduce(f32[256,128]{0,1:T(8,128)S(1)} %bitcast.78), channel_id=1, replica_groups=mesh['dp'=32,'mp'=8] {'mp'}, use_global_device_ids=true, to_apply=%region_7.8 | all-reduce | flops 32768 | bytes 196608 | tf_op jit(solution)/shard_map/psum | solution.py:95
  85.7 0.0 copy-done.2
  85.7 0.9 fusion.19
  86.6 7.1 %all-to-all-start.2 = ((bf16[32,8,512]{2,1,0:T(8,128)(2,1)}), bf16[32,8,512]{2,1,0:T(8,128)(2,1)S(1)}, u32[]{:S(2)}, u32[]{:S(2)}) async-start(bf16[32,8,512]{2,1,0:T(8,128)(2,1)} %fusion.19), calls=%async_computation.2 | async-start | bytes 524288 | tf_op jit(solution)/shard_map/all_to_all | solution.py:101
  93.8 0.0 copy-done.7
  93.8 5.3 %all-to-all-done.2 = bf16[32,8,512]{2,1,0:T(8,128)(2,1)S(1)} async-done(((bf16[32,8,512]{2,1,0:T(8,128)(2,1)}), bf16[32,8,512]{2,1,0:T(8,128)(2,1)S(1)}, u32[]{:S(2)}, u32[]{:S(2)}) %all-to-all-start.2) | async-done | bytes 262176 | tf_op jit(solution)/shard_map/all_to_all | solution.py:101
  99.1 9.4 %all-reduce.3.cloned.1.call-done = f32[128,4096]{1,0:T(8,128)} async-done(((f32[128,4096]{1,0:T(8,128)}), f32[128,4096]{1,0:T(8,128)}) %all-reduce.3.cloned.1.call-update) | async-done | bytes 2097168 | tf_op jit(solution)/shard_map/psum | solution.py:84
  108.5 1.8 %fusion.21 = bf16[128,512]{1,0:T(8,128)(2,1)} fusion(bf16[32,8,512]{2,1,0:T(8,128)(2,1)S(1)} %all-to-all-done.2, f32[128,4096]{1,0:T(8,128)} %all-reduce.3.cloned.1.call-done, s32[]{:T(128)S(6)} %select_n.48, f32[128]{0:T(128)S(1)} %convert_element_type.39, s32[128]{0:T(128)S(1)} %multiply_add_fusion), kind=kOutput, calls=%fused_computation.18 | convolution fusion | flops 33783808 | bytes 656388 | tf_op jit(solution)/shard_map/dot_general | solution.py:102
  (11 shorter events, 0.2 us)
Async XLA Ops:
  6.5 44.6 %copy-start = (bf16[2,1024,64]{1,2,0:T(8,128)(2,1)S(1)}, bf16[2,1024,64]{1,2,0:T(8,128)(2,1)}, u32[]{:S(2)}) copy-start(bf16[2,1024,64]{1,2,0:T(8,128)(2,1)} %param.22) | copy-start | bytes 786436
  6.5 5.5 %copy-start.1 = (bf16[128,8,128]{2,1,0:T(8,128)(2,1)S(1)}, bf16[128,8,128]{2,1,0:T(8,128)(2,1)}, u32[]{:S(2)}) copy-start(bf16[128,8,128]{2,1,0:T(8,128)(2,1)} %param.12) | copy-start | bytes 786436
  6.5 5.5 %copy-start.6 = (bf16[128,1,128]{2,0,1:T(8,128)(2,1)S(1)}, bf16[128,1,128]{2,0,1:T(8,128)(2,1)}, u32[]{:S(2)}) copy-start(bf16[128,1,128]{2,0,1:T(8,128)(2,1)} %param.15) | copy-start | bytes 98308
  6.5 6.7 %copy-start.3 = (bf16[128,1,128]{2,0,1:T(8,128)(2,1)S(1)}, bf16[128,1,128]{2,0,1:T(8,128)(2,1)}, u32[]{:S(2)}) copy-start(bf16[128,1,128]{2,0,1:T(8,128)(2,1)} %param.16) | copy-start | bytes 98308
  6.5 101.9 %all-reduce.3.cloned.1.call-start = ((), (), s32[]{:S(2)}) async-start(), calls=%async_computation.3 | async-start | bytes 4194304 | tf_op jit(solution)/shard_map/psum | solution.py:84
  16.7 6.0 %copy-start.4 = (s32[4096]{0:T(1024)S(1)}, s32[4096]{0:T(1024)}, u32[]{:S(2)}) copy-start(s32[4096]{0:T(1024)} %param.20) | copy-start | bytes 49156
  16.7 6.0 %copy-start.5 = (s32[128]{0:T(128)S(1)}, s32[128]{0:T(128)}, u32[]{:S(2)}) copy-start(s32[128]{0:T(128)} %param.19) | copy-start | bytes 1540
  22.7 63.0 %copy-start.2 = (bf16[2,64,512]{2,1,0:T(8,128)(2,1)S(1)}, bf16[2,64,512]{2,1,0:T(8,128)(2,1)}, u32[]{:S(2)}) copy-start(bf16[2,64,512]{2,1,0:T(8,128)(2,1)} %param.23) | copy-start | bytes 393220
  22.7 71.1 %copy-start.7 = (s32[128]{0:T(128)S(1)}, s32[128]{0:T(128)}, u32[]{:S(2)}) copy-start(s32[128]{0:T(128)} %param.18) | copy-start | bytes 1540
  24.5 11.0 %all-to-all-start = ((s32[32,1,8]{2,1,0:T(1,128)}), s32[32,1,8]{2,1,0:T(1,128)S(1)}, u32[]{:S(2)}, u32[]{:S(2)}) async-start(s32[32,1,8]{2,1,0:T(1,128)} %bitcast.6), calls=%async_computation | async-start | bytes 32768 | tf_op jit(solution)/shard_map/all_to_all | solution.py:87
  35.4 15.7 %all-to-all-start.1 = ((bf16[32,8,1024]{2,1,0:T(8,128)(2,1)}), bf16[32,8,1024]{2,1,0:T(8,128)(2,1)S(1)}, u32[]{:S(2)}, u32[]{:S(2)}) async-start(bf16[32,8,1024]{2,1,0:T(8,128)(2,1)} %fusion.4), calls=%async_computation.1 | async-start | bytes 1048576 | tf_op jit(solution)/shard_map/all_to_all | solution.py:86
  86.6 12.4 %all-to-all-start.2 = ((bf16[32,8,512]{2,1,0:T(8,128)(2,1)}), bf16[32,8,512]{2,1,0:T(8,128)(2,1)S(1)}, u32[]{:S(2)}, u32[]{:S(2)}) async-start(bf16[32,8,512]{2,1,0:T(8,128)(2,1)} %fusion.19), calls=%async_computation.2 | async-start | bytes 524288 | tf_op jit(solution)/shard_map/all_to_all | solution.py:101
Sparse Core Ops, SparseCore 0:
  22.9 85.5 all-reduce.2
where the time goes:
time: 118 us; the launch traced here: 117 us
  blocking collectives  34.2 us (29%)
  waiting for transfers between devices  25.1 us (21%)
  starting transfers between devices  22.2 us (19%)
  matrix products  18.5 us (16%)
  between operations  13.6 us (12%)
  other arithmetic  2.26 us (2%)
  local copies, waits for them, and re-layouts  1.31 us (1%)
    psum x1, blocking collectives, body(): lax.psum(partial_value.reshape(owners_count * capacity, adapters_here * r...  34.2 us
    psum x1, waiting for transfers between devices, body(): full = lax.psum(partial_value, 'mp')  9.39 us
    all_to_all x1, waiting for transfers between devices, body(): lax.all_to_all(send_rows, 'dp', split_axis=0, concat_axis=0, tiled=True)  7.91 us
    all_to_all x1, starting transfers between devices, body(): lax.all_to_all(send_rows, 'dp', split_axis=0, concat_axis=0, tiled=True)  7.63 us
    all_to_all x1, starting transfers between devices, body(): lax.all_to_all(send_ids, 'dp', split_axis=0, concat_axis=0, tiled=True)  7.41 us
    all_to_all x1, starting transfers between devices, body(): back = lax.all_to_all(delta, 'dp', split_axis=0, concat_axis=0, tiled=True)  7.14 us
    dot_general x1, matrix products, body(): jnp.dot(attended, out_weight, preferred_element_type=jnp.float32)  5.97 us
    all_to_all x1, waiting for transfers between devices, body(): back = lax.all_to_all(delta, 'dp', split_axis=0, concat_axis=0, tiled=True)  5.27 us
  transfers between devices with their start and end apart: 4, of which 4 were waited for; matrix products, arithmetic and copies ran while one was open for 3% of the time, Pallas kernels for 0%

commit v1 on v0

--- a/solution.py
+++ b/solution.py
@@ -81,7 +81,7 @@
         slot_code[:, None] == jnp.arange(owners_count * capacity, dtype=jnp.int32)[None, :]
     ).astype(jnp.bfloat16)
     partial_value = jnp.dot(attended, out_weight, preferred_element_type=jnp.float32)
-    full = lax.psum(partial_value, "mp")
+    full = jnp.sum(lax.all_gather(partial_value, "mp"), axis=0)
     base = lax.dynamic_slice_in_dim(full, lax.axis_index("mp") * out_local, out_local, 1)
     got_rows = lax.all_to_all(send_rows, "dp", split_axis=0, concat_axis=0, tiled=True)
     got_ids = lax.all_to_all(send_ids, "dp", split_axis=0, concat_axis=0, tiled=True)

time: 118 us -> 218 us (1.85)
  waiting for transfers between devices: 25.1 us -> 115 us
  other arithmetic: 2.26 us -> 9.7 us
  blocking collectives: 34.2 us -> 36.4 us
    all_gather x0 -> x1, waiting for transfers between devices: none -> 105 us  [body(): full = jnp.sum(lax.all_gather(partial_value, 'mp'), axis=0)]
    psum x1 -> x0, waiting for transfers between devices: 9.39 us -> none  [body(): full = lax.psum(partial_value, 'mp')]
    reduce_sum x0 -> x1, other arithmetic: none -> 7.43 us  [body(): full = jnp.sum(lax.all_gather(partial_value, 'mp'), axis=0)]
    all_to_all x1, waiting for transfers between devices: 5.27 us -> 0.01 us  [body(): back = lax.all_to_all(delta, 'dp', split_axis=0, concat_axis=0, tiled=True)]
    psum x1, blocking collectives: 34.2 us -> 36.4 us  [body(): lax.psum(partial_value.reshape(owners_count * capacity, adapters_here * r...]
  transfers between devices with their start and end apart: 4 -> 4, of which waited for: 4 -> 3; matrix products, arithmetic and copies ran while one was open for 3% -> 5% of each run, Pallas kernels for 0% -> 0%
where the time goes in v1:
time: 218 us; the launch traced here: 216 us
  waiting for transfers between devices  115 us (53%)
  blocking collectives  36.4 us (17%)
  starting transfers between devices  22.2 us (10%)
  matrix products  17.7 us (8%)
  between operations  13.6 us (6%)
  other arithmetic  9.7 us (4%)
    all_gather x1, waiting for transfers between devices, body(): full = jnp.sum(lax.all_gather(partial_value, 'mp'), axis=0)  105 us
    psum x1, blocking collectives, body(): lax.psum(partial_value.reshape(owners_count * capacity, adapters_here * r...  36.4 us
    all_to_all x1, waiting for transfers between devices, body(): lax.all_to_all(send_rows, 'dp', split_axis=0, concat_axis=0, tiled=True)  7.91 us
    all_to_all x1, starting transfers between devices, body(): lax.all_to_all(send_rows, 'dp', split_axis=0, concat_axis=0, tiled=True)  7.63 us
    reduce_sum x1, other arithmetic, body(): full = jnp.sum(lax.all_gather(partial_value, 'mp'), axis=0)  7.43 us
    all_to_all x1, starting transfers between devices, body(): lax.all_to_all(send_ids, 'dp', split_axis=0, concat_axis=0, tiled=True)  7.41 us
    all_to_all x1, starting transfers between devices, body(): back = lax.all_to_all(delta, 'dp', split_axis=0, concat_axis=0, tiled=True)  7.14 us
    dot_general x1, matrix products, body(): jnp.dot(attended, out_weight, preferred_element_type=jnp.float32)  6.02 us
  transfers between devices with their start and end apart: 4, of which 3 were waited for; matrix products, arithmetic and copies ran while one was open for 5% of the time, Pallas kernels for 0%

profile of v1, /device:TPU:22, one launch (start us, length us, event | category | flops | bytes accessed | tf_op | source)
XLA Modules:
  0.0 216.3 jit_solution(15806310068035334202)
XLA Ops:
  6.5 0.0 copy-start
  6.5 0.0 copy-start.1
  6.5 0.0 copy-start.6
  6.5 0.0 copy-start.3
  6.5 0.0 all-gather.3.cloned.1.call-start
  6.6 0.8 iota_compare_fusion.6
  7.4 4.6 %fusion.42 = (f32[128,8]{1,0:T(8,128)S(1)}, f32[128,8,128]{2,1,0:T(8,128)S(1)}) fusion(bf16[128,8,128]{2,1,0:T(8,128)(2,1)} %param.12, bf16[128,1,128,128]{3,2,1,0:T(8,128)(2,1)} %param.13, pred[128,128]{1,0:T(8,128)(4,1)S(1)} %iota_compare_fusion.6), kind=kOutput, calls=%fused_computation.60 | convolution fusion | flops 33946624 | bytes 5001216 | tf_op jit(solution)/shard_map/bgjd,bgtd->bgjt/dot_general | solution.py:15
  12.0 0.1 copy.19
  12.1 0.0 copy-done.1
  12.1 0.0 copy-done.6
  12.1 0.3 fusion.36
  12.4 0.1 copy.20
  12.6 0.4 fusion.24
  13.0 0.1 copy.22
  13.1 0.1 copy.23
  13.2 0.0 copy-done.3
  13.3 3.5 %fusion.16 = bf16[128,8,128]{2,1,0:T(8,128)(2,1)S(1)} fusion(bf16[128,1,128,128]{3,2,1,0:T(8,128)(2,1)} %param.14, f32[128,8,128]{2,1,0:T(8,128)S(1)} %get-tuple-element.10, f32[128,128]{1,0:T(8,128)S(1)} %bitcast_convert_fusion, f32[128,8]{1,0:T(8,128)S(1)} %copy.23, f32[128,8]{1,0:T(8,128)S(1)} %copy.22, f32[128,8]{1,0:T(8,128)S(1)} %copy.20), kind=kOutput, calls=%fused_computation.14 | convolution fusion | flops 34340864 | bytes 5058560 | tf_op jit(solution)/shard_map/bgjt,bgtd->bgjd/dot_general | solution.py:29
  16.7 0.0 copy-start.4
  16.7 0.0 copy-start.5
  16.7 6.0 %fusion.26 = f32[128,4096]{1,0:T(8,128)} fusion(bf16[1024,4096]{1,0:T(8,128)(2,1)} %param.21, bf16[16,8,8,128]{3,2,1,0:T(8,128)(2,1)S(1)} %bitcast.77), kind=kOutput, calls=%fused_computation.25 | convolution fusion | flops 1073741824 | bytes 10747904 | tf_op jit(solution)/shard_map/dot_general | solution.py:83
  22.8 0.0 copy-start.2
  22.8 0.0 copy-start.7
  22.8 0.0 all-gather.3.cloned.1.call-update
  22.8 0.0 copy-done.4
  22.8 0.0 copy-done.5
  22.8 0.4 select_reduce_fusion
  23.3 0.1 fusion.35
  23.4 0.2 reduce_window_sum.11
  23.5 0.2 select_reduce_fusion.2
  23.7 0.1 select_reduce_fusion.1
  23.8 0.7 all_to_all.12
  24.5 7.4 %all-to-all-start = ((s32[32,1,8]{2,1,0:T(1,128)}), s32[32,1,8]{2,1,0:T(1,128)S(1)}, u32[]{:S(2)}, u32[]{:S(2)}) async-start(s32[32,1,8]{2,1,0:T(1,128)} %bitcast.7), calls=%async_computation | async-start | bytes 32768 | tf_op jit(solution)/shard_map/all_to_all | solution.py:87
  32.0 1.1 fusion.4
  33.0 2.5 %all-to-all-done = s32[32,1,8]{2,1,0:T(1,128)S(1)} async-done(((s32[32,1,8]{2,1,0:T(1,128)}), s32[32,1,8]{2,1,0:T(1,128)S(1)}, u32[]{:S(2)}, u32[]{:S(2)}) %all-to-all-start) | async-done | bytes 1056 | tf_op jit(solution)/shard_map/all_to_all | solution.py:87
  35.5 7.6 %all-to-all-start.1 = ((bf16[32,8,1024]{2,1,0:T(8,128)(2,1)}), bf16[32,8,1024]{2,1,0:T(8,128)(2,1)S(1)}, u32[]{:S(2)}, u32[]{:S(2)}) async-start(bf16[32,8,1024]{2,1,0:T(8,128)(2,1)} %fusion.4), calls=%async_computation.1 | async-start | bytes 1048576 | tf_op jit(solution)/shard_map/all_to_all | solution.py:86
  43.2 0.1 sub.34
  43.3 7.9 %all-to-all-done.1 = bf16[32,8,1024]{2,1,0:T(8,128)(2,1)S(1)} async-done(((bf16[32,8,1024]{2,1,0:T(8,128)(2,1)}), bf16[32,8,1024]{2,1,0:T(8,128)(2,1)S(1)}, u32[]{:S(2)}, u32[]{:S(2)}) %all-to-all-start.1) | async-done | bytes 524320 | tf_op jit(solution)/shard_map/all_to_all | solution.py:86
  51.2 0.0 copy-done
  51.2 0.3 fusion.22
  51.5 36.4 %all-reduce.1 = bf16[256,128]{0,1:T(8,128)(2,1)S(1)} all-reduce(f32[256,128]{0,1:T(8,128)S(1)} %bitcast.80), channel_id=1, replica_groups=mesh['dp'=32,'mp'=8] {'mp'}, use_global_device_ids=true, to_apply=%region_7.8 | all-reduce | flops 32768 | bytes 196608 | tf_op jit(solution)/shard_map/psum | solution.py:95
  88.0 0.0 copy-done.2
  88.0 1.0 fusion.19
  88.9 7.1 %all-to-all-start.2 = ((bf16[32,8,512]{2,1,0:T(8,128)(2,1)}), bf16[32,8,512]{2,1,0:T(8,128)(2,1)S(1)}, u32[]{:S(2)}, u32[]{:S(2)}) async-start(bf16[32,8,512]{2,1,0:T(8,128)(2,1)} %fusion.19), calls=%async_computation.2 | async-start | bytes 524288 | tf_op jit(solution)/shard_map/all_to_all | solution.py:101
  96.1 0.0 copy-done.7
  96.1 105.0 %all-gather.3.cloned.1.call-done = f32[1024,4096]{1,0:T(8,128)} async-done(((f32[128,4096]{1,0:T(8,128)}), f32[1024,4096]{1,0:T(8,128)}) %all-gather.3.cloned.1.call-update) | async-done | bytes 16777232 | tf_op jit(solution)/shard_map/all_gather | solution.py:84
  201.1 7.4 %reduce_sum.46 = f32[128,4096]{1,0:T(8,128)S(1)} reduce(f32[8,128,4096]{2,1,0:T(8,128)} %bitcast.76, f32[]{:T(128)} %constant.43.clone.1), dimensions={0}, to_apply=%region_2.3 | reduce | flops 3670016 | bytes 18874372 | tf_op jit(solution)/shard_map/reduce_sum | solution.py:84
  208.5 0.0 all-to-all-done.2
  208.5 0.9 fusion.21
  (11 shorter events, 0.2 us)
Async XLA Ops:
  6.5 44.7 %copy-start = (bf16[2,1024,64]{1,2,0:T(8,128)(2,1)S(1)}, bf16[2,1024,64]{1,2,0:T(8,128)(2,1)}, u32[]{:S(2)}) copy-start(bf16[2,1024,64]{1,2,0:T(8,128)(2,1)} %param.22) | copy-start | bytes 786436
  6.5 5.5 %copy-start.1 = (bf16[128,8,128]{2,1,0:T(8,128)(2,1)S(1)}, bf16[128,8,128]{2,1,0:T(8,128)(2,1)}, u32[]{:S(2)}) copy-start(bf16[128,8,128]{2,1,0:T(8,128)(2,1)} %param.12) | copy-start | bytes 786436
  6.5 5.5 %copy-start.6 = (bf16[128,1,128]{2,0,1:T(8,128)(2,1)S(1)}, bf16[128,1,128]{2,0,1:T(8,128)(2,1)}, u32[]{:S(2)}) copy-start(bf16[128,1,128]{2,0,1:T(8,128)(2,1)} %param.15) | copy-start | bytes 98308
  6.5 6.7 %copy-start.3 = (bf16[128,1,128]{2,0,1:T(8,128)(2,1)S(1)}, bf16[128,1,128]{2,0,1:T(8,128)(2,1)}, u32[]{:S(2)}) copy-start(bf16[128,1,128]{2,0,1:T(8,128)(2,1)} %param.16) | copy-start | bytes 98308
  6.5 194.5 %all-gather.3.cloned.1.call-start = ((), (), s32[]{:S(2)}) async-start(), calls=%async_computation.3 | async-start | bytes 18874368 | tf_op jit(solution)/shard_map/all_gather | solution.py:84
  16.7 6.1 %copy-start.4 = (s32[4096]{0:T(1024)S(1)}, s32[4096]{0:T(1024)}, u32[]{:S(2)}) copy-start(s32[4096]{0:T(1024)} %param.20) | copy-start | bytes 49156
  16.7 6.1 %copy-start.5 = (s32[128]{0:T(128)S(1)}, s32[128]{0:T(128)}, u32[]{:S(2)}) copy-start(s32[128]{0:T(128)} %param.19) | copy-start | bytes 1540
  22.8 65.2 %copy-start.2 = (bf16[2,64,512]{2,1,0:T(8,128)(2,1)S(1)}, bf16[2,64,512]{2,1,0:T(8,128)(2,1)}, u32[]{:S(2)}) copy-start(bf16[2,64,512]{2,1,0:T(8,128)(2,1)} %param.23) | copy-start | bytes 393220
  22.8 73.3 %copy-start.7 = (s32[128]{0:T(128)S(1)}, s32[128]{0:T(128)}, u32[]{:S(2)}) copy-start(s32[128]{0:T(128)} %param.18) | copy-start | bytes 1540
  24.5 11.0 %all-to-all-start = ((s32[32,1,8]{2,1,0:T(1,128)}), s32[32,1,8]{2,1,0:T(1,128)S(1)}, u32[]{:S(2)}, u32[]{:S(2)}) async-start(s32[32,1,8]{2,1,0:T(1,128)} %bitcast.7), calls=%async_computation | async-start | bytes 32768 | tf_op jit(solution)/shard_map/all_to_all | solution.py:87
  35.5 15.7 %all-to-all-start.1 = ((bf16[32,8,1024]{2,1,0:T(8,128)(2,1)}), bf16[32,8,1024]{2,1,0:T(8,128)(2,1)S(1)}, u32[]{:S(2)}, u32[]{:S(2)}) async-start(bf16[32,8,1024]{2,1,0:T(8,128)(2,1)} %fusion.4), calls=%async_computation.1 | async-start | bytes 1048576 | tf_op jit(solution)/shard_map/all_to_all | solution.py:86
  88.9 119.6 %all-to-all-start.2 = ((bf16[32,8,512]{2,1,0:T(8,128)(2,1)}), bf16[32,8,512]{2,1,0:T(8,128)(2,1)S(1)}, u32[]{:S(2)}, u32[]{:S(2)}) async-start(bf16[32,8,512]{2,1,0:T(8,128)(2,1)} %fusion.19), calls=%async_computation.2 | async-start | bytes 524288 | tf_op jit(solution)/shard_map/all_to_all | solution.py:101
Sparse Core Ops, SparseCore 0:
  22.9 178.1 all-gather.2
